TPU v7x, 512 devices: a whole 4x8x8 slice. The times are simulated.
512 devices in a mesh: dp: 2 (over core), ctx: 64 (over z, y), head: 4 (over x).
Axes of the slice: x: 4, y: 8, z: 8, core: 2. Of those that a mesh axis runs over, the one named last changes fastest.
Arguments:
- queries: bfloat16 [2, 8192, 2560], P('dp', 'ctx', 'head'), may hold values from -25 to 25
- keys: bfloat16 [2, 8192, 2560], P('dp', 'ctx', 'head'), may hold values from -25 to 25
- values: bfloat16 [2, 8192, 2560], P('dp', 'ctx', 'head'), may hold values from -6 to 6
- grad_y: bfloat16 [2, 8192, 2560], P('dp', 'ctx', 'head'), may hold values from -6 to 6
- out_gain: float32 [2560], P('head'), may hold values from 0.1 to 1.9
- offsets: int32 [2, 20], P(None, 'head'), may hold values from 0 to 63, as said below
Outputs:
- attended: bfloat16 [2, 8192, 2560], P('dp', 'ctx', 'head')
- query_grad: bfloat16 [2, 8192, 2560], P('dp', 'ctx', 'head')
- key_grad: bfloat16 [2, 8192, 2560], P('dp', 'ctx', 'head')
- value_grad: bfloat16 [2, 8192, 2560], P('dp', 'ctx', 'head')
- gain_grad: float32 [2560], P('head')
Inputs may be any that keep to these rules, and one draw needn't show every extreme that they name: Row 0 holds offsets below 8, row 1 offsets below 64.
All inputs are finite; a program needn't handle non-finite values.
Results may differ from a plain program's by a relative error of at most 0.011.
Values may be sent and summed in bfloat16 or wider, within the bound.
A program may use at most 64 MiB of HBM per device.

v0:
```python
import math
import jax
import jax.numpy as jnp
from jax import lax
from jax.sharding import PartitionSpec as P

HEAD_DIM = 128
SPAN = 4
R1 = 8
EPS = 1e-06


def group_gather(block, axis, group):
    count = lax.axis_size(axis)
    pieces = [block]
    for shift in range(1, group):
        route = []
        for src in range(count):
            base = src - src % group
            route.append((src, base + (src % group + shift) % group))
        pieces.append(lax.ppermute(block, axis, route))
    return jnp.concatenate(pieces, 0)


def pick_rows(source_rows, dilation, shifts):
    row_count, head_count, head_width = source_rows.shape
    grouped = source_rows.reshape(row_count // dilation, dilation, head_count, head_width)
    hit_mask = jnp.arange(dilation, dtype=jnp.int32).reshape(1, dilation, 1, 1) == shifts.reshape(
        1, 1, head_count, 1
    )
    chosen = jnp.where(hit_mask, grouped, jnp.zeros((), source_rows.dtype))
    return jnp.sum(chosen, axis=1, dtype=source_rows.dtype)


def place_rows(row_values, dilation, shifts):
    row_count, head_count, head_width = row_values.shape
    hit_mask = jnp.arange(dilation, dtype=jnp.int32).reshape(1, dilation, 1, 1) == shifts.reshape(
        1, 1, head_count, 1
    )
    spread = jnp.where(hit_mask, row_values[:, None], jnp.zeros((), row_values.dtype))
    return spread.reshape(row_count * dilation, head_count, head_width)


def level_scores(q_rows, k_rows):
    score_scale = 1.0 / math.sqrt(q_rows.shape[-1])
    return (
        jnp.einsum("qhe,khe->hqk", q_rows, k_rows, preferred_element_type=jnp.float32) * score_scale
    )


def attend(q_rows, k_rows, v_rows):
    scores = level_scores(q_rows, k_rows)
    row_max = jnp.max(scores, axis=-1, keepdims=True)
    log_total = row_max[..., 0] + jnp.log(jnp.sum(jnp.exp(scores - row_max), axis=-1))
    soft_rows = jnp.exp(scores - log_total[..., None]).astype(jnp.bfloat16)
    level_out = jnp.einsum("hqk,khe->qhe", soft_rows, v_rows, preferred_element_type=jnp.float32)
    return (level_out, log_total.T)


def score_grads(q_rows, k_rows, v_rows, log_total, grad_low, row_shift):
    score_scale = 1.0 / math.sqrt(q_rows.shape[-1])
    scores = level_scores(q_rows, k_rows)
    exact_soft = jnp.exp(scores - log_total.T[..., None])
    prob_grad = jnp.einsum("qhe,khe->hqk", grad_low, v_rows, preferred_element_type=jnp.float32)
    score_grad = (exact_soft * (prob_grad + row_shift.T[..., None]) * score_scale).astype(
        jnp.bfloat16
    )
    return (score_grad, exact_soft.astype(jnp.bfloat16))


def key_parts(score_grad, soft_low, q_rows, grad_low):
    k_part = jnp.einsum("hqk,qhe->khe", score_grad, q_rows, preferred_element_type=jnp.float32)
    v_part = jnp.einsum("hqk,qhe->khe", soft_low, grad_low, preferred_element_type=jnp.float32)
    return (k_part, v_part)


def query_part(score_grad, k_rows):
    return jnp.einsum("hqk,khe->qhe", score_grad, k_rows, preferred_element_type=jnp.float32)


def split_qkv(packed, head_count):
    width = head_count * HEAD_DIM
    shape = (packed.shape[0], head_count, HEAD_DIM)
    return tuple((packed[:, i * width : (i + 1) * width].reshape(shape) for i in range(3)))


def pack_grads(grad_low, row_shift):
    rows = grad_low.shape[0]
    return jnp.concatenate(
        [grad_low.astype(jnp.float32).reshape(rows, -1), row_shift.astype(jnp.float32)], 1
    )


def unpack_grads(packed, head_count):
    width = head_count * HEAD_DIM
    grad_low = packed[:, :width].astype(jnp.bfloat16).reshape(-1, head_count, HEAD_DIM)
    return (grad_low, packed[:, width:])


def shards(queries, keys, values, grad_y, out_gain, offsets):
    tokens = queries.shape[1]
    flat_width = queries.shape[2]
    head_count = flat_width // HEAD_DIM
    row_shape = (tokens, head_count, HEAD_DIM)
    q_own = queries[0].reshape(row_shape)
    k_own = keys[0].reshape(row_shape)
    v_own = values[0].reshape(row_shape)
    ctx_size = lax.axis_size("ctx")
    my_place = lax.axis_index("ctx")
    mid_shift = offsets[0]
    top_shift = offsets[1]
    positions = jnp.arange(tokens, dtype=jnp.int32)
    mid_hit = (positions % R1)[:, None] == mid_shift[None, :]
    top_hit = (positions % ctx_size)[:, None] == top_shift[None, :]
    mid_pack = jnp.concatenate(
        [pick_rows(x, R1, mid_shift).reshape(-1, flat_width) for x in (q_own, k_own, v_own)], 1
    )
    top_pack = jnp.concatenate(
        [pick_rows(x, ctx_size, top_shift).reshape(-1, flat_width) for x in (q_own, k_own, v_own)],
        1,
    )
    mid_rows = mid_pack.shape[0]
    top_rows = top_pack.shape[0]
    mid_all = group_gather(mid_pack, "ctx", SPAN)
    top_all = lax.all_gather(top_pack, "ctx", axis=0, tiled=True)
    mid_q, mid_k, mid_v = split_qkv(mid_all, head_count)
    top_q, top_k, top_v = split_qkv(top_all, head_count)
    top_start = my_place * top_rows
    base_out, base_total = attend(q_own, k_own, v_own)
    mid_out_all, mid_total_all = attend(mid_q, mid_k, mid_v)
    top_out_all, top_total_all = attend(top_q, top_k, top_v)
    mid_out = mid_out_all[:mid_rows]
    mid_total = mid_total_all[:mid_rows]
    top_out = lax.dynamic_slice_in_dim(top_out_all, top_start, top_rows, 0)
    top_total = lax.dynamic_slice_in_dim(top_total_all, top_start, top_rows, 0)
    mid_full = place_rows(mid_total[..., None], R1, mid_shift)[..., 0]
    top_full = place_rows(top_total[..., None], ctx_size, top_shift)[..., 0]
    row_max = jnp.maximum(base_total, jnp.where(mid_hit, mid_full, base_total))
    row_max = jnp.maximum(row_max, jnp.where(top_hit, top_full, base_total))
    base_expo = jnp.exp(base_total - row_max)
    mid_expo = jnp.where(mid_hit, jnp.exp(mid_full - row_max), 0.0)
    top_expo = jnp.where(top_hit, jnp.exp(top_full - row_max), 0.0)
    denom = base_expo + mid_expo + top_expo
    base_share = base_expo / denom
    mid_share = mid_expo / denom
    top_share = top_expo / denom
    attn = (
        base_share[..., None] * base_out
        + mid_share[..., None] * place_rows(mid_out, R1, mid_shift)
        + top_share[..., None] * place_rows(top_out, ctx_size, top_shift)
    )
    inv_rms = lax.rsqrt(jnp.mean(attn * attn, axis=-1, keepdims=True) + EPS)
    normed = attn * inv_rms
    gain_rows = out_gain.reshape(head_count, HEAD_DIM)
    attended = (normed * gain_rows).astype(jnp.bfloat16).reshape(1, tokens, flat_width)
    grad_full = grad_y[0].reshape(row_shape).astype(jnp.float32)
    gain_part = jnp.sum(grad_full * normed, axis=0).reshape(flat_width)
    grad_norm = grad_full * gain_rows
    grad_attn = inv_rms * (
        grad_norm - normed * jnp.mean(grad_norm * normed, axis=-1, keepdims=True)
    )
    inner = jnp.sum(grad_attn * attn, axis=-1)
    base_low = (base_share[..., None] * grad_attn).astype(jnp.bfloat16)
    base_shift = -(base_share * inner)
    base_grad, base_soft = score_grads(q_own, k_own, v_own, base_total, base_low, base_shift)
    base_dq = query_part(base_grad, k_own)
    base_dk, base_dv = key_parts(base_grad, base_soft, q_own, base_low)
    mid_sel = pick_rows(mid_share[..., None], R1, mid_shift)[..., 0]
    mid_low = (mid_sel[..., None] * pick_rows(grad_attn, R1, mid_shift)).astype(jnp.bfloat16)
    mid_row_shift = -(mid_sel * pick_rows(inner[..., None], R1, mid_shift)[..., 0])
    top_sel = pick_rows(top_share[..., None], ctx_size, top_shift)[..., 0]
    top_low = (top_sel[..., None] * pick_rows(grad_attn, ctx_size, top_shift)).astype(jnp.bfloat16)
    top_row_shift = -(top_sel * pick_rows(inner[..., None], ctx_size, top_shift)[..., 0])
    mid_low_all, mid_shift_all = unpack_grads(
        group_gather(pack_grads(mid_low, mid_row_shift), "ctx", SPAN), head_count
    )
    top_grads = pack_grads(top_low, top_row_shift)
    gain_row = jnp.pad(gain_part, (0, top_grads.shape[1] - flat_width))[None]
    gathered = lax.all_gather(jnp.concatenate([top_grads, gain_row], 0), "ctx", axis=0)
    top_low_all, top_shift_all = unpack_grads(
        gathered[:, :top_rows].reshape(-1, top_grads.shape[1]), head_count
    )
    gain_grad = lax.psum(jnp.sum(gathered[:, top_rows, :flat_width], axis=0), "dp")
    mid_grad, mid_soft = score_grads(mid_q, mid_k, mid_v, mid_total_all, mid_low_all, mid_shift_all)
    mid_dq = query_part(mid_grad[:, :mid_rows], mid_k)
    mid_dk, mid_dv = key_parts(
        mid_grad[:, :, :mid_rows], mid_soft[:, :, :mid_rows], mid_q, mid_low_all
    )
    top_grad, top_soft = score_grads(top_q, top_k, top_v, top_total_all, top_low_all, top_shift_all)
    own_grad = lax.dynamic_slice_in_dim(top_grad, top_start, top_rows, 1)
    top_dq = query_part(own_grad, top_k)
    key_grad_cols = lax.dynamic_slice_in_dim(top_grad, top_start, top_rows, 2)
    key_soft_cols = lax.dynamic_slice_in_dim(top_soft, top_start, top_rows, 2)
    top_dk, top_dv = key_parts(key_grad_cols, key_soft_cols, top_q, top_low_all)
    query_grad = (
        base_dq + place_rows(mid_dq, R1, mid_shift) + place_rows(top_dq, ctx_size, top_shift)
    )
    key_grad = base_dk + place_rows(mid_dk, R1, mid_shift) + place_rows(top_dk, ctx_size, top_shift)
    value_grad = (
        base_dv + place_rows(mid_dv, R1, mid_shift) + place_rows(top_dv, ctx_size, top_shift)
    )
    out_shape = (1, tokens, flat_width)
    return (
        attended,
        query_grad.astype(jnp.bfloat16).reshape(out_shape),
        key_grad.astype(jnp.bfloat16).reshape(out_shape),
        value_grad.astype(jnp.bfloat16).reshape(out_shape),
        gain_grad,
    )


def solution(mesh):
    in_specs = (
        P("dp", "ctx", "head"),
        P("dp", "ctx", "head"),
        P("dp", "ctx", "head"),
        P("dp", "ctx", "head"),
        P("head"),
        P(None, "head"),
    )
    out_specs = (
        P("dp", "ctx", "head"),
        P("dp", "ctx", "head"),
        P("dp", "ctx", "head"),
        P("dp", "ctx", "head"),
        P("head"),
    )
    return jax.shard_map(shards, mesh=mesh, in_specs=in_specs, out_specs=out_specs, check_vma=False)
```

profile of v0, /device:TPU:1, one launch (start us, length us, event | category | flops | bytes accessed | tf_op | source)
XLA Modules:
  0.0 159.5 jit_solution(9887099655481750333)
XLA Ops:
  0.6 0.8 slice_bitcast_fusion.5
  1.5 1.5 fusion.24
  3.0 6.1 %collective-permute-start.2 = (bf16[16,1920]{1,0:T(8,128)(2,1)S(1)}, bf16[16,1920]{1,0:T(8,128)(2,1)S(1)}, u32[]{:S(2)}, u32[]{:S(2)}) collective-permute-start(bf16[16,1920]{1,0:T(8,128)(2,1)S(1)} %bitcast_dynamic-update-slice_fusion), channel_id=1, source_target_pairs={{0,12},{4,0},{8,4},{12,8},{16,28},{20,16},{24,20},{28,24},{32,44},... | collective-permute-start | bytes 184328 | tf_op jit(solution)/shard_map/ppermute | solution.py:21
  9.1 1.9 %collective-permute-start.1 = (bf16[16,1920]{1,0:T(8,128)(2,1)S(1)}, bf16[16,1920]{1,0:T(8,128)(2,1)S(1)}, u32[]{:S(2)}, u32[]{:S(2)}) collective-permute-start(bf16[16,1920]{1,0:T(8,128)(2,1)S(1)} %bitcast_dynamic-update-slice_fusion), channel_id=1, source_target_pairs={{0,8},{4,12},{8,0},{12,4},{16,24},{20,28},{24,16},{28,20},{32,40},... | collective-permute-start | bytes 184328 | tf_op jit(solution)/shard_map/ppermute | solution.py:21
  11.0 2.3 %collective-permute-start = (bf16[16,1920]{1,0:T(8,128)(2,1)S(1)}, bf16[16,1920]{1,0:T(8,128)(2,1)S(1)}, u32[]{:S(2)}, u32[]{:S(2)}) collective-permute-start(bf16[16,1920]{1,0:T(8,128)(2,1)S(1)} %bitcast_dynamic-update-slice_fusion), channel_id=1, source_target_pairs={{0,4},{4,8},{8,12},{12,0},{16,20},{20,24},{24,28},{28,16},{32,36},... | collective-permute-start | bytes 184328 | tf_op jit(solution)/shard_map/ppermute | solution.py:21
  13.6 0.7 copy-done.1
  14.5 0.7 copy-done.2
  16.4 0.3 copy-done.8
  17.4 44.2 %all-gather.1 = bf16[64,2,1920]{2,1,0:T(2,128)(2,1)S(1)} all-gather(bf16[1,2,1920]{2,1,0:T(2,128)(2,1)S(1)} %maximum_bitcast_fusion.2), channel_id=1, replica_groups=mesh['dp'=2,'ctx'=64,'head'=4] {'ctx'}, dimensions={0}, use_global_device_ids=true | all-gather | bytes 499200 | tf_op jit(solution)/shard_map/all_gather | solution.py:125
  65.3 0.5 multiply_reduce_fusion.3
  65.8 0.7 copy-done.9
  66.5 0.8 multiply_reduce_fusion.2
  68.2 0.6 pad_maximum_fusion.2
  68.9 3.9 %collective-permute-start.5 = (f32[16,645]{1,0:T(8,128)}, f32[16,645]{1,0:T(8,128)}, u32[]{:S(2)}, u32[]{:S(2)}) collective-permute-start(f32[16,645]{1,0:T(8,128)} %pad_maximum_fusion.2), channel_id=1, source_target_pairs={{0,12},{4,0},{8,4},{12,8},{16,28},{20,16},{24,20},{28,24},{32,44},... | collective-permute-start | bytes 123848 | tf_op jit(solution)/shard_map/ppermute | solution.py:21
  72.8 2.8 %collective-permute-start.4 = (f32[16,645]{1,0:T(8,128)}, f32[16,645]{1,0:T(8,128)}, u32[]{:S(2)}, u32[]{:S(2)}) collective-permute-start(f32[16,645]{1,0:T(8,128)} %pad_maximum_fusion.2), channel_id=1, source_target_pairs={{0,8},{4,12},{8,0},{12,4},{16,24},{20,28},{24,16},{28,20},{32,40},... | collective-permute-start | bytes 123848 | tf_op jit(solution)/shard_map/ppermute | solution.py:21
  75.6 1.9 %collective-permute-start.3 = (f32[16,645]{1,0:T(8,128)}, f32[16,645]{1,0:T(8,128)}, u32[]{:S(2)}, u32[]{:S(2)}) collective-permute-start(f32[16,645]{1,0:T(8,128)} %pad_maximum_fusion.2), channel_id=1, source_target_pairs={{0,4},{4,8},{8,12},{12,0},{16,20},{20,24},{24,28},{28,16},{32,36},... | collective-permute-start | bytes 123848 | tf_op jit(solution)/shard_map/ppermute | solution.py:21
  78.2 38.9 %all-gather.2 = f32[64,3,645]{2,1,0:T(4,128)S(1)} all-gather(f32[1,3,645]{2,1,0:T(4,128)S(1)} %maximum_bitcast_fusion.1), channel_id=2, replica_groups=mesh['dp'=2,'ctx'=64,'head'=4] {'ctx'}, dimensions={0}, use_global_device_ids=true | all-gather | bytes 503100 | tf_op jit(solution)/shard_map/all_gather | solution.py:179
  117.2 1.0 reshape.365
  118.2 0.8 slice_bitcast_fusion.3
  119.1 1.0 slice.110
  120.3 0.9 convolution_bitcast_fusion.9
  121.7 0.4 convolution_bitcast_fusion.8
  122.1 0.4 fusion.17
  122.7 0.7 copy-done.4
  123.5 0.8 copy.357
  124.5 28.0 %psum.7 = f32[640]{0:T(1024)} all-reduce(f32[640]{0:T(1024)S(1)} %slice_reduce_fusion), channel_id=1, replica_groups=mesh['dp'=2,'ctx'=64,'head'=4] {'dp'}, use_global_device_ids=true, to_apply=%region_23.24 | all-reduce | flops 640 | bytes 5120 | tf_op jit(solution)/shard_map/psum | solution.py:183
  152.5 0.9 pad_maximum_fusion.1
  153.4 0.9 convolution_bitcast_fusion.5
  154.2 0.8 maximum_bitcast_fusion
  156.1 0.8 copy.359
  157.4 0.8 copy.358
  158.7 0.8 copy.360
  (114 shorter events, 10.7 us)
Async XLA Ops:
  1.5 11.9 %copy-start = (bf16[1,128,640]{2,1,0:T(8,128)(2,1)S(1)}, bf16[1,128,640]{2,1,0:T(8,128)(2,1)}, u32[]{:S(2)}) copy-start(bf16[1,128,640]{2,1,0:T(8,128)(2,1)} %param.6) | copy-start | bytes 491524
  3.0 60.7 %collective-permute-start.2 = (bf16[16,1920]{1,0:T(8,128)(2,1)S(1)}, bf16[16,1920]{1,0:T(8,128)(2,1)S(1)}, u32[]{:S(2)}, u32[]{:S(2)}) collective-permute-start(bf16[16,1920]{1,0:T(8,128)(2,1)S(1)} %bitcast_dynamic-update-slice_fusion), channel_id=1, source_target_pairs={{0,12},{4,0},{8,4},{12,8},{16,28},{20,16},{24,20},{28,24},{32,44},... | collective-permute-start | bytes 184328 | tf_op jit(solution)/shard_map/ppermute | solution.py:21
  9.1 54.7 %collective-permute-start.1 = (bf16[16,1920]{1,0:T(8,128)(2,1)S(1)}, bf16[16,1920]{1,0:T(8,128)(2,1)S(1)}, u32[]{:S(2)}, u32[]{:S(2)}) collective-permute-start(bf16[16,1920]{1,0:T(8,128)(2,1)S(1)} %bitcast_dynamic-update-slice_fusion), channel_id=1, source_target_pairs={{0,8},{4,12},{8,0},{12,4},{16,24},{20,28},{24,16},{28,20},{32,40},... | collective-permute-start | bytes 184328 | tf_op jit(solution)/shard_map/ppermute | solution.py:21
  11.0 52.7 %collective-permute-start = (bf16[16,1920]{1,0:T(8,128)(2,1)S(1)}, bf16[16,1920]{1,0:T(8,128)(2,1)S(1)}, u32[]{:S(2)}, u32[]{:S(2)}) collective-permute-start(bf16[16,1920]{1,0:T(8,128)(2,1)S(1)} %bitcast_dynamic-update-slice_fusion), channel_id=1, source_target_pairs={{0,4},{4,8},{8,12},{12,0},{16,20},{20,24},{24,28},{28,16},{32,36},... | collective-permute-start | bytes 184328 | tf_op jit(solution)/shard_map/ppermute | solution.py:21
  13.4 0.9 copy-start.1
  14.3 0.9 copy-start.2
  15.8 0.9 copy-start.8
  62.7 0.7 copy-start.3
  63.8 0.6 copy-start.6
  64.1 0.6 copy-start.5
  65.8 0.7 copy-start.9
  68.9 83.7 %collective-permute-start.5 = (f32[16,645]{1,0:T(8,128)}, f32[16,645]{1,0:T(8,128)}, u32[]{:S(2)}, u32[]{:S(2)}) collective-permute-start(f32[16,645]{1,0:T(8,128)} %pad_maximum_fusion.2), channel_id=1, source_target_pairs={{0,12},{4,0},{8,4},{12,8},{16,28},{20,16},{24,20},{28,24},{32,44},... | collective-permute-start | bytes 123848 | tf_op jit(solution)/shard_map/ppermute | solution.py:21
  72.8 79.7 %collective-permute-start.4 = (f32[16,645]{1,0:T(8,128)}, f32[16,645]{1,0:T(8,128)}, u32[]{:S(2)}, u32[]{:S(2)}) collective-permute-start(f32[16,645]{1,0:T(8,128)} %pad_maximum_fusion.2), channel_id=1, source_target_pairs={{0,8},{4,12},{8,0},{12,4},{16,24},{20,28},{24,16},{28,20},{32,40},... | collective-permute-start | bytes 123848 | tf_op jit(solution)/shard_map/ppermute | solution.py:21
  75.6 76.9 %collective-permute-start.3 = (f32[16,645]{1,0:T(8,128)}, f32[16,645]{1,0:T(8,128)}, u32[]{:S(2)}, u32[]{:S(2)}) collective-permute-start(f32[16,645]{1,0:T(8,128)} %pad_maximum_fusion.2), channel_id=1, source_target_pairs={{0,4},{4,8},{8,12},{12,0},{16,20},{20,24},{24,28},{28,16},{32,36},... | collective-permute-start | bytes 123848 | tf_op jit(solution)/shard_map/ppermute | solution.py:21
  122.4 0.9 copy-start.4
  154.2 1.0 copy-start.7
where the time goes:
time: 160 us
  blocking collectives  111 us (69%)
  starting transfers between devices  19 us (12%)
  local copies, waits for them, and re-layouts  15.2 us (10%)
  other arithmetic  7.09 us (4%)
  matrix products  6.04 us (4%)
    all_gather x1, blocking collectives, shards(): top_all = lax.all_gather(top_pack, 'ctx', axis=0, tiled=True)  44.2 us
    all_gather x1, blocking collectives, shards(): lax.all_gather(jnp.concatenate([top_grads, gain_row], 0), 'ctx', axis=0)  38.9 us
    psum x1, blocking collectives, shards(): lax.psum(jnp.sum(gathered[:, top_rows, :flat_width], axis=0), 'dp')  28 us
    ppermute x6, starting transfers between devices, group_gather(): pieces.append(lax.ppermute(block, axis, route))  19 us
    unnamed x34, local copies, waits for them, and re-layouts  7.85 us
  transfers between devices with their start and end apart: 6, of which 0 were waited for; matrix products, arithmetic and copies ran while one was open for 7% of the time, Pallas kernels for 0%

commit v1 on v0

--- a/solution.py
+++ b/solution.py
@@ -8,6 +8,11 @@
 SPAN = 4
 R1 = 8
 EPS = 1e-06
+
+
+def tiled_gather(shard, axis, dim):
+    copies = jnp.concatenate([shard] * lax.axis_size(axis), axis=dim)
+    return lax.all_to_all(copies, axis, dim, dim, tiled=True)
 
 
 def group_gather(block, axis, group):
@@ -122,7 +127,7 @@
     mid_rows = mid_pack.shape[0]
     top_rows = top_pack.shape[0]
     mid_all = group_gather(mid_pack, "ctx", SPAN)
-    top_all = lax.all_gather(top_pack, "ctx", axis=0, tiled=True)
+    top_all = tiled_gather(top_pack, "ctx", 0)
     mid_q, mid_k, mid_v = split_qkv(mid_all, head_count)
     top_q, top_k, top_v = split_qkv(top_all, head_count)
     top_start = my_place * top_rows

time: 160 us -> 136 us (0.85)
  blocking collectives: 111 us -> 55.8 us
  starting transfers between devices: 19 us -> 34.9 us
  waiting for transfers between devices: 0.02 us -> 11.6 us
  local copies, waits for them, and re-layouts: 15.2 us -> 18.3 us
    all_gather x1 -> x0, blocking collectives: 44.2 us -> none  [shards(): top_all = lax.all_gather(top_pack, 'ctx', axis=0, tiled=True)]
    all_to_all x0 -> x1, starting transfers between devices: none -> 14.6 us  [tiled_gather(): return lax.all_to_all(copies, axis, dim, dim, tiled=True)]
    all_to_all x0 -> x1, waiting for transfers between devices: none -> 11.6 us  [tiled_gather(): return lax.all_to_all(copies, axis, dim, dim, tiled=True)]
    psum x1, blocking collectives: 28 us -> 18.7 us  [shards(): lax.psum(jnp.sum(gathered[:, top_rows, :flat_width], axis=0), 'dp')]
    all_gather x1, blocking collectives: 38.9 us -> 37.1 us  [shards(): lax.all_gather(jnp.concatenate([top_grads, gain_row], 0), 'ctx', axis=0)]
    unnamed x34 -> x49, local copies, waits for them, and re-layouts: 7.85 us -> 8.77 us
  transfers between devices with their start and end apart: 6 -> 7, of which waited for: 0 -> 1; matrix products, arithmetic and copies ran while one was open for 7% -> 9% of each run, Pallas kernels for 0% -> 0%
where the time goes in v1:
time: 136 us
  blocking collectives  55.8 us (41%)
  starting transfers between devices  34.9 us (26%)
  local copies, waits for them, and re-layouts  18.3 us (13%)
  waiting for transfers between devices  11.6 us (9%)
  other arithmetic  7.6 us (6%)
  matrix products  6.05 us (4%)
    all_gather x1, blocking collectives, shards(): lax.all_gather(jnp.concatenate([top_grads, gain_row], 0), 'ctx', axis=0)  37.1 us
    ppermute x6, starting transfers between devices, group_gather(): pieces.append(lax.ppermute(block, axis, route))  20.3 us
    psum x1, blocking collectives, shards(): lax.psum(jnp.sum(gathered[:, top_rows, :flat_width], axis=0), 'dp')  18.7 us
    all_to_all x1, starting transfers between devices, tiled_gather(): return lax.all_to_all(copies, axis, dim, dim, tiled=True)  14.6 us
    all_to_all x1, waiting for transfers between devices, tiled_gather(): return lax.all_to_all(copies, axis, dim, dim, tiled=True)  11.6 us
    unnamed x49, local copies, waits for them, and re-layouts  8.77 us
  transfers between devices with their start and end apart: 7, of which 1 were waited for; matrix products, arithmetic and copies ran while one was open for 9% of the time, Pallas kernels for 0%

profile of v1, /device:TPU:1, one launch (start us, length us, event | category | flops | bytes accessed | tf_op | source)
XLA Modules:
  0.0 135.5 jit_solution(14557936050875243890)
XLA Ops:
  0.6 0.8 slice_bitcast_fusion.5
  1.4 0.5 copy-done.12
  2.0 1.5 %fusion.24 = (bf16[16,5,128]{2,0,1:T(8,128)(2,1)S(1)}, bf16[16,5,128]{2,0,1:T(8,128)(2,1)S(1)}, bf16[16,5,128]{2,0,1:T(8,128)(2,1)S(1)}) fusion(pred[8,5]{0,1:T(8,128)(4,1)S(1)} %iota_compare_fusion.1, bf16[1,128,640]{2,1,0:T(8,128)(2,1)} %param.6, bf16[1,128,640]{2,1,0:T(8,128)(2,1)} %param.7, bf16[1,128,640]{2,1,0:T(8,128)(2,1)} %param.8), kind=kLoop, calls=%fused_computation.70 | loop fusion | flops 460800 | bytes 553000 | tf_op jit(solution)/shard_map/reduce_sum | solution.py:37
  3.6 6.2 %collective-permute-start.2 = (bf16[16,1920]{1,0:T(8,128)(2,1)S(1)}, bf16[16,1920]{1,0:T(8,128)(2,1)S(1)}, u32[]{:S(2)}, u32[]{:S(2)}) collective-permute-start(bf16[16,1920]{1,0:T(8,128)(2,1)S(1)} %bitcast_dynamic-update-slice_fusion), channel_id=1, source_target_pairs={{0,12},{4,0},{8,4},{12,8},{16,28},{20,16},{24,20},{28,24},{32,44},... | collective-permute-start | bytes 184328 | tf_op jit(solution)/shard_map/ppermute | solution.py:26
  9.8 1.9 %collective-permute-start.1 = (bf16[16,1920]{1,0:T(8,128)(2,1)S(1)}, bf16[16,1920]{1,0:T(8,128)(2,1)S(1)}, u32[]{:S(2)}, u32[]{:S(2)}) collective-permute-start(bf16[16,1920]{1,0:T(8,128)(2,1)S(1)} %bitcast_dynamic-update-slice_fusion), channel_id=1, source_target_pairs={{0,8},{4,12},{8,0},{12,4},{16,24},{20,28},{24,16},{28,20},{32,40},... | collective-permute-start | bytes 184328 | tf_op jit(solution)/shard_map/ppermute | solution.py:26
  11.7 2.3 %collective-permute-start = (bf16[16,1920]{1,0:T(8,128)(2,1)S(1)}, bf16[16,1920]{1,0:T(8,128)(2,1)S(1)}, u32[]{:S(2)}, u32[]{:S(2)}) collective-permute-start(bf16[16,1920]{1,0:T(8,128)(2,1)S(1)} %bitcast_dynamic-update-slice_fusion), channel_id=1, source_target_pairs={{0,4},{4,8},{8,12},{12,0},{16,20},{20,24},{24,28},{28,16},{32,36},... | collective-permute-start | bytes 184328 | tf_op jit(solution)/shard_map/ppermute | solution.py:26
  14.5 0.7 copy-done.2
  15.9 1.0 concatenate.27
  17.0 1.0 all_to_all.8
  17.9 14.6 %all-to-all-start = ((bf16[64,2,1920]{2,1,0:T(2,128)(2,1)}), bf16[64,2,1920]{2,1,0:T(2,128)(2,1)S(1)}, u32[]{:S(2)}, u32[]{:S(2)}) async-start(bf16[64,2,1920]{2,1,0:T(2,128)(2,1)} %all_to_all.8), calls=%async_computation | async-start | bytes 983040 | tf_op jit(solution)/shard_map/all_to_all | solution.py:15
  33.3 0.5 copy-done.8
  36.2 11.6 %all-to-all-done = bf16[64,2,1920]{2,1,0:T(2,128)(2,1)S(1)} async-done(((bf16[64,2,1920]{2,1,0:T(2,128)(2,1)}), bf16[64,2,1920]{2,1,0:T(2,128)(2,1)S(1)}, u32[]{:S(2)}, u32[]{:S(2)}) %all-to-all-start) | async-done | bytes 491552 | tf_op jit(solution)/shard_map/all_to_all | solution.py:15
  51.3 0.7 copy-done.9
  51.9 0.8 multiply_reduce_fusion.2
  53.7 0.6 pad_maximum_fusion.2
  54.3 5.3 %collective-permute-start.5 = (f32[16,645]{1,0:T(8,128)}, f32[16,645]{1,0:T(8,128)}, u32[]{:S(2)}, u32[]{:S(2)}) collective-permute-start(f32[16,645]{1,0:T(8,128)} %pad_maximum_fusion.2), channel_id=1, source_target_pairs={{0,12},{4,0},{8,4},{12,8},{16,28},{20,16},{24,20},{28,24},{32,44},... | collective-permute-start | bytes 123848 | tf_op jit(solution)/shard_map/ppermute | solution.py:26
  59.6 1.9 %collective-permute-start.4 = (f32[16,645]{1,0:T(8,128)}, f32[16,645]{1,0:T(8,128)}, u32[]{:S(2)}, u32[]{:S(2)}) collective-permute-start(f32[16,645]{1,0:T(8,128)} %pad_maximum_fusion.2), channel_id=1, source_target_pairs={{0,8},{4,12},{8,0},{12,4},{16,24},{20,28},{24,16},{28,20},{32,40},... | collective-permute-start | bytes 123848 | tf_op jit(solution)/shard_map/ppermute | solution.py:26
  61.5 2.6 %collective-permute-start.3 = (f32[16,645]{1,0:T(8,128)}, f32[16,645]{1,0:T(8,128)}, u32[]{:S(2)}, u32[]{:S(2)}) collective-permute-start(f32[16,645]{1,0:T(8,128)} %pad_maximum_fusion.2), channel_id=1, source_target_pairs={{0,4},{4,8},{8,12},{12,0},{16,20},{20,24},{24,28},{28,16},{32,36},... | collective-permute-start | bytes 123848 | tf_op jit(solution)/shard_map/ppermute | solution.py:26
  65.2 37.1 %all-gather.1 = f32[64,3,645]{2,1,0:T(4,128)S(1)} all-gather(f32[1,3,645]{2,1,0:T(4,128)S(1)} %maximum_bitcast_fusion.1), channel_id=2, replica_groups=mesh['dp'=2,'ctx'=64,'head'=4] {'ctx'}, dimensions={0}, use_global_device_ids=true | all-gather | bytes 503100 | tf_op jit(solution)/shard_map/all_gather | solution.py:184
  102.4 1.0 reshape.367
  103.4 0.8 slice_bitcast_fusion.3
  104.3 1.0 slice.110
  105.5 0.9 convolution_bitcast_fusion.9
  107.9 0.7 copy-done.4
  108.8 0.8 copy.289
  109.8 18.7 %psum.7 = f32[640]{0:T(1024)} all-reduce(f32[640]{0:T(1024)S(1)} %slice_reduce_fusion), channel_id=1, replica_groups=mesh['dp'=2,'ctx'=64,'head'=4] {'dp'}, use_global_device_ids=true, to_apply=%region_23.24 | all-reduce | flops 640 | bytes 5120 | tf_op jit(solution)/shard_map/psum | solution.py:188
  128.5 0.9 pad_maximum_fusion.1
  129.4 0.9 convolution_bitcast_fusion.5
  130.2 0.8 maximum_bitcast_fusion
  132.1 0.8 copy.291
  133.4 0.8 copy.290
  134.7 0.8 copy.292
  (133 shorter events, 13.6 us)
Async XLA Ops:
  1.4 0.5 copy-start.12
  1.4 14.0 %copy-start.14 = (s32[5]{0:T(128)}, s32[5]{0:T(128)S(1)}, u32[]{:S(2)}) copy-start(s32[5]{0:T(128)S(1)} %get-tuple-element.57) | copy-start | bytes 64
  2.0 12.1 %copy-start = (bf16[1,128,640]{2,1,0:T(8,128)(2,1)S(1)}, bf16[1,128,640]{2,1,0:T(8,128)(2,1)}, u32[]{:S(2)}) copy-start(bf16[1,128,640]{2,1,0:T(8,128)(2,1)} %param.6) | copy-start | bytes 491524
  3.6 10.7 %copy-start.1 = (bf16[1,128,640]{2,1,0:T(8,128)(2,1)S(1)}, bf16[1,128,640]{2,1,0:T(8,128)(2,1)}, u32[]{:S(2)}) copy-start(bf16[1,128,640]{2,1,0:T(8,128)(2,1)} %param.7) | copy-start | bytes 491524
  3.6 31.4 %collective-permute-start.2 = (bf16[16,1920]{1,0:T(8,128)(2,1)S(1)}, bf16[16,1920]{1,0:T(8,128)(2,1)S(1)}, u32[]{:S(2)}, u32[]{:S(2)}) collective-permute-start(bf16[16,1920]{1,0:T(8,128)(2,1)S(1)} %bitcast_dynamic-update-slice_fusion), channel_id=1, source_target_pairs={{0,12},{4,0},{8,4},{12,8},{16,28},{20,16},{24,20},{28,24},{32,44},... | collective-permute-start | bytes 184328 | tf_op jit(solution)/shard_map/ppermute | solution.py:26
  9.8 25.2 %collective-permute-start.1 = (bf16[16,1920]{1,0:T(8,128)(2,1)S(1)}, bf16[16,1920]{1,0:T(8,128)(2,1)S(1)}, u32[]{:S(2)}, u32[]{:S(2)}) collective-permute-start(bf16[16,1920]{1,0:T(8,128)(2,1)S(1)} %bitcast_dynamic-update-slice_fusion), channel_id=1, source_target_pairs={{0,8},{4,12},{8,0},{12,4},{16,24},{20,28},{24,16},{28,20},{32,40},... | collective-permute-start | bytes 184328 | tf_op jit(solution)/shard_map/ppermute | solution.py:26
  11.7 23.3 %collective-permute-start = (bf16[16,1920]{1,0:T(8,128)(2,1)S(1)}, bf16[16,1920]{1,0:T(8,128)(2,1)S(1)}, u32[]{:S(2)}, u32[]{:S(2)}) collective-permute-start(bf16[16,1920]{1,0:T(8,128)(2,1)S(1)} %bitcast_dynamic-update-slice_fusion), channel_id=1, source_target_pairs={{0,4},{4,8},{8,12},{12,0},{16,20},{20,24},{24,28},{28,16},{32,36},... | collective-permute-start | bytes 184328 | tf_op jit(solution)/shard_map/ppermute | solution.py:26
  14.3 0.9 copy-start.2
  15.5 17.6 %copy-start.10 = (pred[64,5]{0,1:T(8,128)(4,1)}, pred[64,5]{0,1:T(8,128)(4,1)S(1)}, u32[]{:S(2)}) copy-start(pred[64,5]{0,1:T(8,128)(4,1)S(1)} %iota_compare_fusion) | copy-start | bytes 964
  17.9 29.9 %all-to-all-start = ((bf16[64,2,1920]{2,1,0:T(2,128)(2,1)}), bf16[64,2,1920]{2,1,0:T(2,128)(2,1)S(1)}, u32[]{:S(2)}, u32[]{:S(2)}) async-start(bf16[64,2,1920]{2,1,0:T(2,128)(2,1)} %all_to_all.8), calls=%async_computation | async-start | bytes 983040 | tf_op jit(solution)/shard_map/all_to_all | solution.py:15
  32.9 0.9 copy-start.8
  35.1 0.6 copy-start.6
  35.5 0.6 copy-start.5
  48.9 0.6 copy-start.17
  49.0 1.5 %copy-start.3 = (bf16[5,128,128]{1,2,0:T(8,128)(2,1)}, bf16[5,128,128]{1,2,0:T(8,128)(2,1)S(1)}, u32[]{:S(2)}) copy-start(bf16[5,128,128]{1,2,0:T(8,128)(2,1)S(1)} %fusion.23) | copy-start | bytes 491524
  49.2 0.6 copy-start.13
  49.2 0.7 copy-start.15
  49.2 0.7 copy-start.16
  51.2 0.7 copy-start.9
  54.3 74.2 %collective-permute-start.5 = (f32[16,645]{1,0:T(8,128)}, f32[16,645]{1,0:T(8,128)}, u32[]{:S(2)}, u32[]{:S(2)}) collective-permute-start(f32[16,645]{1,0:T(8,128)} %pad_maximum_fusion.2), channel_id=1, source_target_pairs={{0,12},{4,0},{8,4},{12,8},{16,28},{20,16},{24,20},{28,24},{32,44},... | collective-permute-start | bytes 123848 | tf_op jit(solution)/shard_map/ppermute | solution.py:26
  59.6 68.9 %collective-permute-start.4 = (f32[16,645]{1,0:T(8,128)}, f32[16,645]{1,0:T(8,128)}, u32[]{:S(2)}, u32[]{:S(2)}) collective-permute-start(f32[16,645]{1,0:T(8,128)} %pad_maximum_fusion.2), channel_id=1, source_target_pairs={{0,8},{4,12},{8,0},{12,4},{16,24},{20,28},{24,16},{28,20},{32,40},... | collective-permute-start | bytes 123848 | tf_op jit(solution)/shard_map/ppermute | solution.py:26
  61.5 67.0 %collective-permute-start.3 = (f32[16,645]{1,0:T(8,128)}, f32[16,645]{1,0:T(8,128)}, u32[]{:S(2)}, u32[]{:S(2)}) collective-permute-start(f32[16,645]{1,0:T(8,128)} %pad_maximum_fusion.2), channel_id=1, source_target_pairs={{0,4},{4,8},{8,12},{12,0},{16,20},{20,24},{24,28},{28,16},{32,36},... | collective-permute-start | bytes 123848 | tf_op jit(solution)/shard_map/ppermute | solution.py:26
  64.1 0.7 copy-start.11
  107.7 0.9 copy-start.4
  130.2 1.0 copy-start.7
